TPU v7x, 128 devices: a whole 4x4x4 slice. The times are simulated.
128 devices in a mesh: tiles: 16 (over y, z), nests: 8 (over x, core).
Axes of the slice: x: 4, y: 4, z: 4, core: 2. Of those that a mesh axis runs over, the one named last changes fastest.
Arguments:
- parent: float32 [1024, 2048, 128], P('tiles', 'nests'), may hold values from -6 to 6
- nest_state: float32 [8, 64, 128, 128], P('nests', 'tiles'), may hold values from -6 to 6
- parent_mix: float32 [128, 128], replicated, may hold values from -0.24 to 0.24
- nest_mix: float32 [128, 128], replicated, may hold values from -0.24 to 0.24
- courant: float32 [2, 128], replicated, may hold values from 0.05 to 0.45
- nest_pos: int32 [8, 2], P('nests'), may hold values from 0 to 5954, as said below
Outputs:
- parent_out: float32 [1024, 2048, 128], P('tiles', 'nests')
- nest_out: float32 [8, 64, 128, 128], P('nests', 'tiles')
Inputs may be any that keep to these rules, and one draw needn't show every extreme that they name: nest_pos[n] = (3 i + a, 3 q + c) with a, c in 0..2, i <= 1001, and n * 256 <= q <= (n + 1) * 256 - 64: nest n reads and feeds only parent columns of the n-th group of 256 columns.
All inputs are finite; a program needn't handle non-finite values.
Results may differ from a plain program's by a relative error of at most 0.0003.
Values sent between devices are 32-bit elements; how exact they have to be, the bound alone decides.
No kernel may reach another device: no remote copies, remote signals or barrier semaphores. Data moves between devices by JAX's collectives and lax.ppermute only.
A program may use at most 128 MiB of HBM per device.

v0:
```python
import jax
import jax.numpy as jnp
from jax import lax
from jax.sharding import PartitionSpec as P

BLK = 64
STEPS = 3
KAPPA = 0.125
HIGH = lax.Precision.HIGHEST


def with_halo(block, sides, width):
    for axis, dim in sides:
        count = lax.axis_size(axis)
        forward = [(i, i + 1) for i in range(count - 1)]
        backward = [(target, source) for source, target in forward]
        low = lax.ppermute(
            lax.slice_in_dim(block, block.shape[dim] - width, None, axis=dim), axis, forward
        )
        high = lax.ppermute(lax.slice_in_dim(block, 0, width, axis=dim), axis, backward)
        block = jnp.concatenate([low, block, high], axis=dim)
    return block


def passed_along(block, axis, distance):
    devices = range(lax.axis_size(axis))
    route = [(i - distance, i) for i in devices if i - distance in devices]
    return lax.ppermute(block, axis, route)


def nest_advance(current, upper, edge, courant, nest_mix):
    left = jnp.concatenate([edge, current[:, :-1]], axis=1)
    mixed = jnp.einsum("xyc,cd->xyd", current, nest_mix, precision=HIGH)
    return current + courant[0] * (upper - current) + courant[1] * (left - current) + mixed


def bilinear(data, anchor, rows, columns_count, block_len):
    cols = jnp.arange(columns_count, dtype=jnp.int32)
    spot = anchor[1] + cols
    near = spot // 3 - anchor[1] // 3
    frac_y = (spot % 3).astype(jnp.float32) / 3.0
    places = jnp.arange(block_len, dtype=jnp.int32)[None, :]
    zero = jnp.zeros((columns_count, block_len), jnp.float32)
    table = jnp.where(places == near[:, None], (1.0 - frac_y)[:, None] + zero, zero)
    table = table + jnp.where(places == near[:, None] + 1, frac_y[:, None] + zero, zero)
    frac_x = ((anchor[0] + rows) % 3).astype(jnp.float32) / 3.0
    upper_part = jnp.einsum("nb,xbc->xnc", table, data[:, 0], precision=HIGH)
    lower_part = jnp.einsum("nb,xbc->xnc", table, data[:, 1], precision=HIGH)
    return (1.0 - frac_x)[:, None, None] * upper_part + frac_x[:, None, None] * lower_part


def shards(parent, nest_state, parent_mix, nest_mix, courant, nest_pos):
    tile_rows, tile_cols, width = parent.shape
    nest_rows = nest_state.shape[1]
    nest_cols = nest_state.shape[2]
    tiles_count = lax.axis_size("tiles")
    slots = (nest_rows + 1) // 3 + 2
    tile_index = lax.axis_index("tiles")
    column_index = lax.axis_index("nests")
    anchor = nest_pos[0]
    corner = anchor[1] // 3
    base = tile_index * nest_rows
    lowest = (anchor[0] + base) // 3
    strip = lax.dynamic_slice_in_dim(parent, corner - column_index * tile_cols, BLK, 1)
    receivers = jnp.arange(tiles_count, dtype=jnp.int32)
    wanted = ((anchor[0] + receivers * nest_rows) // 3)[:, None] + jnp.arange(
        slots, dtype=jnp.int32
    )[None, :]
    local = wanted - tile_index * tile_rows
    inside = (local >= 0) & (local < tile_rows)
    taken = strip[jnp.clip(local, 0, tile_rows - 1)]
    local_rows = lax.psum_scatter(
        jnp.where(inside[..., None, None], taken, 0.0), "tiles", scatter_dimension=0, tiled=True
    ).reshape(slots, BLK, width)
    padded = with_halo(parent, (("tiles", 0), ("nests", 1)), 1)
    beside_all = padded[2:, 1:-1] + padded[:-2, 1:-1] + padded[1:-1, 2:] + padded[1:-1, :-2]
    mixed = jnp.einsum("xyc,cd->xyd", parent, parent_mix, precision=HIGH)
    parent_new = parent + KAPPA * (beside_all - 4.0 * parent) + mixed
    rows = base + jnp.arange(nest_rows, dtype=jnp.int32)
    near_row = (anchor[0] + rows) // 3 - lowest
    data = jnp.stack([local_rows[near_row], local_rows[near_row + 1]], axis=1)
    interp = bilinear(data, anchor, rows, nest_cols, BLK)
    start = 0.5 * (nest_state[0] + interp)
    first = tile_index == 0
    edge = start[:, :1]
    current = start
    for step in range(STEPS):
        above = passed_along(current[-1:], "tiles", 1)
        above = jnp.where(first, start[:1], above)
        upper = jnp.concatenate([above, current[:-1]], axis=0)
        current = nest_advance(current, upper, edge, courant, nest_mix)
    fb_rows = (nest_rows + 2) // 3
    fb_cols = (nest_cols + 2) // 3
    counter = jnp.arange(fb_rows, dtype=jnp.int32)
    ys = -anchor[1] % 3 + 3 * jnp.arange(fb_cols, dtype=jnp.int32)
    col_live = ys < nest_cols
    xs = base + -(anchor[0] + base) % 3 + 3 * counter
    row_live = xs < base + nest_rows
    own_values = current[jnp.clip(xs - base, 0, nest_rows - 1)][:, jnp.clip(ys, 0, nest_cols - 1)]
    own_values = jnp.where((row_live[:, None] & col_live[None, :])[..., None], own_values, 0.0)
    pcol = (anchor[1] + ys) // 3 - column_index * tile_cols
    col_ok = col_live & (pcol >= 0) & (pcol < tile_cols)
    piece = lax.all_gather(own_values, "tiles", axis=0, tiled=True)
    slot_index = jnp.arange(piece.shape[0], dtype=jnp.int32)
    sender = slot_index // fb_rows
    sender_base = sender * nest_rows
    sender_x = sender_base + -(anchor[0] + sender_base) % 3 + 3 * (slot_index % fb_rows)
    prow = (anchor[0] + sender_x) // 3 - tile_index * tile_rows
    row_ok = (sender_x < sender_base + nest_rows) & (prow >= 0) & (prow < tile_rows)
    valid = row_ok[:, None] & col_ok[None, :]
    old = parent_new[
        jnp.clip(prow, 0, tile_rows - 1)[:, None], jnp.clip(pcol, 0, tile_cols - 1)[None, :]
    ]
    diff = jnp.where(valid[..., None], 0.5 * (piece - old), 0.0)
    row_index = jnp.where(valid, prow[:, None], tile_rows)
    col_index = jnp.broadcast_to(jnp.clip(pcol, 0, tile_cols - 1)[None, :], valid.shape)
    parent_out = parent_new.at[row_index, col_index].add(diff, mode="drop")
    return (parent_out, current[None])


def solution(mesh):
    placed = (
        P("tiles", "nests", None),
        P("nests", "tiles", None, None),
        P(),
        P(),
        P(),
        P("nests", None),
    )
    return jax.shard_map(
        shards,
        mesh=mesh,
        in_specs=placed,
        out_specs=(P("tiles", "nests", None), P("nests", "tiles", None, None)),
        check_vma=False,
    )
```

profile of v0, /device:TPU:6, one launch (start us, length us, event | category | flops | bytes accessed | tf_op | source)
XLA Modules:
  0.0 216.7 jit_solution(3485163505775321891)
XLA Ops:
  7.2 0.0 copy-start
  7.2 0.0 copy-start.6
  7.2 0.0 copy-start.5
  7.2 0.0 reduce-scatter.4.cloned.1.call-start
  7.3 1.0 fusion.71
  8.3 3.8 %collective-permute-start.1 = (f32[1,256,128]{2,1,0:T(8,128)S(1)}, f32[1,256,128]{2,1,0:T(8,128)S(1)}, u32[]{:S(2)}, u32[]{:S(2)}) collective-permute-start(f32[1,256,128]{2,1,0:T(8,128)S(1)} %get-tuple-element.13), channel_id=1, source_target_pairs={{0,8},{8,16},{16,24},{24,32},{32,40},{40,48},{48,56},{56,64},{64,7... | collective-permute-start | bytes 393224 | tf_op jit(solution)/shard_map/ppermute | solution.py:17
  12.1 1.3 collective-permute-start
  13.4 1.3 fusion.72
  17.3 0.7 and_select_fusion.3
  18.0 0.1 compare_select_fusion.1
  18.1 0.1 fusion.44
  18.1 2.0 constant_dynamic-slice_fusion
  20.2 0.1 reshape.533
  20.3 1.8 gather_fusion
  22.0 2.7 %broadcast_select_fusion = f32[16,3,64,128]{3,2,1,0:T(8,128)} fusion(f32[16,3,64,128]{3,2,1,0:T(8,128)} %bitcast.60, pred[16,3]{1,0:T(8,128)(4,1)S(1)} %fusion.44), kind=kLoop, calls=%fused_computation.28 | loop fusion | flops 393216 | bytes 3145776 | tf_op jit(solution)/shard_map/jit(_where)/select_n | solution.py:73
  24.8 0.0 reduce-scatter.4.cloned.1.call-update
  24.8 0.7 clamp_shift-left_fusion
  25.5 0.7 fusion.58
  26.1 0.7 compare_and_fusion
  27.5 0.7 broadcast_subtract_fusion.1
  28.1 0.7 fusion.52
  28.8 0.6 broadcast_add_fusion
  29.5 0.7 fusion.53
  30.2 0.7 compare_and_fusion.1
  30.9 0.1 compare_select_fusion
  31.0 0.1 multiply_reduce_fusion
  31.1 0.1 and_reduce_fusion
  31.2 0.1 broadcast_and_fusion.1
  31.2 0.1 broadcast_and_fusion
  31.3 0.1 broadcast_or_fusion
  31.4 0.1 reshape.577
  31.5 0.1 reshape.571
  31.6 0.0 collective-permute-done.1
  31.6 0.7 constant_dynamic-update-slice_fusion.2
  32.3 7.7 %constant_dynamic-update-slice_fusion.1 = f32[66,256,128]{2,1,0:T(8,128)} fusion(f32[66,256,128]{2,1,0:T(8,128)} %constant_dynamic-update-slice_fusion.2, f32[64,256,128]{2,1,0:T(8,128)} %param.6), kind=kLoop, calls=%fused_computation.88 | loop fusion | bytes 16777216
  40.0 61.8 %reduce-scatter.4.cloned.1.call-done = f32[1,3,64,128]{3,2,1,0:T(8,128)} async-done(((f32[16,3,64,128]{3,2,1,0:T(8,128)}), f32[1,3,64,128]{3,2,1,0:T(8,128)}) %reduce-scatter.4.cloned.1.call-update) | async-done | bytes 98320
  101.8 1.4 gather_fusion.1
  103.2 1.4 gather_fusion.2
  104.7 0.4 convolution_multiply_fusion.1
  105.1 0.5 fusion.10
  105.6 3.1 %collective-permute-start.4 = (f32[1,128,128]{2,1,0:T(8,128)S(1)}, f32[1,128,128]{2,1,0:T(8,128)S(1)}, u32[]{:S(2)}, u32[]{:S(2)}) collective-permute-start(f32[1,128,128]{2,1,0:T(8,128)S(1)} %slice.129), channel_id=1, source_target_pairs={{0,8},{8,16},{16,24},{24,32},{32,40},{40,48},{48,56},{56,64},{64,7... | collective-permute-start | bytes 196616 | tf_op jit(solution)/shard_map/ppermute | solution.py:28
  108.7 0.0 collective-permute-done
  108.7 0.7 constant_dynamic-update-slice_fusion
  109.4 1.2 collective-permute-done.4
  110.6 0.4 convolution_add_fusion.2
  111.0 4.3 %collective-permute-start.5 = (f32[1,128,128]{2,1,0:T(8,128)S(1)}, f32[1,128,128]{2,1,0:T(8,128)S(1)}, u32[]{:S(2)}, u32[]{:S(2)}) collective-permute-start(f32[1,128,128]{2,1,0:T(8,128)S(1)} %slice.133), channel_id=1, source_target_pairs={{0,8},{8,16},{16,24},{24,32},{32,40},{40,48},{48,56},{56,64},{64,7... | collective-permute-start | bytes 196616 | tf_op jit(solution)/shard_map/ppermute | solution.py:28
  115.3 1.1 fusion.70
  116.3 1.9 collective-permute-start.3
  118.3 3.6 %collective-permute-start.2 = (f32[66,1,128]{2,1,0:T(1,128)S(1)}, f32[66,1,128]{2,1,0:T(1,128)S(1)}, u32[]{:S(2)}, u32[]{:S(2)}) collective-permute-start(f32[66,1,128]{2,1,0:T(1,128)S(1)} %get-tuple-element.10), channel_id=1, source_target_pairs={{1,0},{2,1},{3,2},{4,3},{5,4},{6,5},{7,6},{9,8},{10,9},{11,10},{12... | collective-permute-start | bytes 101384 | tf_op jit(solution)/shard_map/ppermute | solution.py:20
  122.0 0.4 convolution_add_fusion.1
  122.4 3.3 %collective-permute-start.6 = (f32[1,128,128]{2,1,0:T(8,128)S(1)}, f32[1,128,128]{2,1,0:T(8,128)S(1)}, u32[]{:S(2)}, u32[]{:S(2)}) collective-permute-start(f32[1,128,128]{2,1,0:T(8,128)S(1)} %slice.136), channel_id=1, source_target_pairs={{0,8},{8,16},{16,24},{24,32},{32,40},{40,48},{48,56},{56,64},{64,7... | collective-permute-start | bytes 196616 | tf_op jit(solution)/shard_map/ppermute | solution.py:28
  125.7 27.0 %fusion.4 = f32[64,256,128]{2,1,0:T(8,128)} fusion(f32[64,256,128]{2,1,0:T(8,128)} %param.6, f32[66,256,128]{2,1,0:T(8,128)} %constant_dynamic-update-slice_fusion, f32[66,1,128]{2,1,0:T(1,128)S(1)} %collective-permute-done.3, f32[66,1,128]{2,1,0:T(1,128)S(1)} %collective-permute-done.2, f32[1,256,128]{2,1,0:T(8,128)S(1)} %collective-permute-done.1, ...), kind=kOutput, calls=%fused_computation.12 | convolution fusion | flops 3246391296 | bytes 25823232 | tf_op jit(solution)/shard_map/xyc,cd->xyd/dot_general | solution.py:77
  152.7 14.5 %gather_fusion.5 = f32[1376,128]{1,0:T(8,128)S(1)} fusion(f32[64,256,128]{2,1,0:T(8,128)} %fusion.4, s32[1376]{0:T(1024)S(1)} %reshape.571), kind=kCustom, calls=%fused_computation.5 | custom fusion | bytes 1420032 | tf_op jit(solution)/shard_map/gather | solution.py:111
  167.2 0.1 reshape.574
  167.3 0.4 convolution_add_fusion
  167.7 0.0 copy-start.2
  167.7 0.6 gather_fusion.3
  168.3 0.1 copy.11
  168.4 0.6 gather_fusion.4
  169.0 0.1 bitcast_select_fusion
  169.2 25.4 %all_gather.3 = f32[32,43,128]{2,1,0:T(8,128)S(1)} all-gather(f32[2,43,128]{2,1,0:T(8,128)S(1)} %copy.12), channel_id=1, replica_groups=mesh['tiles'=16,'nests'=8] {'tiles'}, dimensions={0}, use_global_device_ids=true | all-gather | bytes 748544 | tf_op jit(solution)/shard_map/all_gather | solution.py:103
  194.6 0.3 multiply_select_fusion
  194.9 0.1 reshape.579
  195.0 14.9 %scatter_fusion = f32[16384,128]{1,0:T(8,128)} fusion(f32[16384,128]{1,0:T(8,128)} %bitcast.58, s32[1376]{0:T(1024)S(1)} %reshape.577, f32[1376,128]{1,0:T(8,128)S(1)} %reshape.579), kind=kCustom, calls=%fused_computation.6 | custom fusion | flops 176128 | bytes 2119040
  (38 shorter events, 0.2 us)
Async XLA Ops:
  7.2 118.5 %copy-start = (f32[128,128]{1,0:T(8,128)S(1)}, f32[128,128]{1,0:T(8,128)}, u32[]{:S(2)}) copy-start(f32[128,128]{1,0:T(8,128)} %param.8) | copy-start | bytes 196612
  7.2 23.8 %copy-start.6 = (s32[2]{0:T(128)S(1)}, s32[2]{0:T(128)}, u32[]{:S(2)}) copy-start(s32[2]{0:T(128)} %constant.162) | copy-start | bytes 28
  7.2 23.9 %copy-start.5 = (s32[2]{0:T(128)S(1)}, s32[2]{0:T(128)}, u32[]{:S(2)}) copy-start(s32[2]{0:T(128)} %constant.165) | copy-start | bytes 28
  7.2 23.9 %copy-start.4 = (f32[2,128]{1,0:T(2,128)S(1)}, f32[2,128]{1,0:T(2,128)}, u32[]{:S(2)}) copy-start(f32[2,128]{1,0:T(2,128)} %param.10) | copy-start | bytes 3076
  7.2 94.6 %reduce-scatter.4.cloned.1.call-start = ((), (), s32[]{:S(2)}) async-start(), calls=%async_computation.1 | async-start | bytes 1671168
  8.3 23.4 %collective-permute-start.1 = (f32[1,256,128]{2,1,0:T(8,128)S(1)}, f32[1,256,128]{2,1,0:T(8,128)S(1)}, u32[]{:S(2)}, u32[]{:S(2)}) collective-permute-start(f32[1,256,128]{2,1,0:T(8,128)S(1)} %get-tuple-element.13), channel_id=1, source_target_pairs={{0,8},{8,16},{16,24},{24,32},{32,40},{40,48},{48,56},{56,64},{64,7... | collective-permute-start | bytes 393224 | tf_op jit(solution)/shard_map/ppermute | solution.py:17
  12.1 96.6 %collective-permute-start = (f32[1,256,128]{2,1,0:T(8,128)S(1)}, f32[1,256,128]{2,1,0:T(8,128)S(1)}, u32[]{:S(2)}, u32[]{:S(2)}) collective-permute-start(f32[1,256,128]{2,1,0:T(8,128)S(1)} %get-tuple-element.12), channel_id=1, source_target_pairs={{8,0},{16,8},{24,16},{32,24},{40,32},{48,40},{56,48},{64,56},{72,6... | collective-permute-start | bytes 393224 | tf_op jit(solution)/shard_map/ppermute | solution.py:20
  32.3 72.8 %copy-start.3 = (f32[1,4,128,128]{3,2,1,0:T(8,128)S(1)}, f32[1,4,128,128]{3,2,1,0:T(8,128)}, u32[]{:S(2)}) copy-start(f32[1,4,128,128]{3,2,1,0:T(8,128)} %param.7) | copy-start | bytes 786436
  32.3 78.3 %copy-start.1 = (f32[128,128]{1,0:T(8,128)S(1)}, f32[128,128]{1,0:T(8,128)}, u32[]{:S(2)}) copy-start(f32[128,128]{1,0:T(8,128)} %param.9) | copy-start | bytes 196612
  105.6 5.0 %collective-permute-start.4 = (f32[1,128,128]{2,1,0:T(8,128)S(1)}, f32[1,128,128]{2,1,0:T(8,128)S(1)}, u32[]{:S(2)}, u32[]{:S(2)}) collective-permute-start(f32[1,128,128]{2,1,0:T(8,128)S(1)} %slice.129), channel_id=1, source_target_pairs={{0,8},{8,16},{16,24},{24,32},{32,40},{40,48},{48,56},{56,64},{64,7... | collective-permute-start | bytes 196616 | tf_op jit(solution)/shard_map/ppermute | solution.py:28
  111.0 11.0 %collective-permute-start.5 = (f32[1,128,128]{2,1,0:T(8,128)S(1)}, f32[1,128,128]{2,1,0:T(8,128)S(1)}, u32[]{:S(2)}, u32[]{:S(2)}) collective-permute-start(f32[1,128,128]{2,1,0:T(8,128)S(1)} %slice.133), channel_id=1, source_target_pairs={{0,8},{8,16},{16,24},{24,32},{32,40},{40,48},{48,56},{56,64},{64,7... | collective-permute-start | bytes 196616 | tf_op jit(solution)/shard_map/ppermute | solution.py:28
  116.3 9.3 %collective-permute-start.3 = (f32[66,1,128]{2,1,0:T(1,128)S(1)}, f32[66,1,128]{2,1,0:T(1,128)S(1)}, u32[]{:S(2)}, u32[]{:S(2)}) collective-permute-start(f32[66,1,128]{2,1,0:T(1,128)S(1)} %get-tuple-element.11), channel_id=1, source_target_pairs={{0,1},{1,2},{2,3},{3,4},{4,5},{5,6},{6,7},{8,9},{9,10},{10,11},{11... | collective-permute-start | bytes 101384 | tf_op jit(solution)/shard_map/ppermute | solution.py:17
  118.3 7.4 %collective-permute-start.2 = (f32[66,1,128]{2,1,0:T(1,128)S(1)}, f32[66,1,128]{2,1,0:T(1,128)S(1)}, u32[]{:S(2)}, u32[]{:S(2)}) collective-permute-start(f32[66,1,128]{2,1,0:T(1,128)S(1)} %get-tuple-element.10), channel_id=1, source_target_pairs={{1,0},{2,1},{3,2},{4,3},{5,4},{6,5},{7,6},{9,8},{10,9},{11,10},{12... | collective-permute-start | bytes 101384 | tf_op jit(solution)/shard_map/ppermute | solution.py:20
  122.4 45.0 %collective-permute-start.6 = (f32[1,128,128]{2,1,0:T(8,128)S(1)}, f32[1,128,128]{2,1,0:T(8,128)S(1)}, u32[]{:S(2)}, u32[]{:S(2)}) collective-permute-start(f32[1,128,128]{2,1,0:T(8,128)S(1)} %slice.136), channel_id=1, source_target_pairs={{0,8},{8,16},{16,24},{24,32},{32,40},{40,48},{48,56},{56,64},{64,7... | collective-permute-start | bytes 196616 | tf_op jit(solution)/shard_map/ppermute | solution.py:28
  167.7 42.2 %copy-start.2 = (f32[4,128,128]{2,1,0:T(8,128)}, f32[4,128,128]{2,1,0:T(8,128)S(1)}, u32[]{:S(2)}) copy-start(f32[4,128,128]{2,1,0:T(8,128)S(1)} %convolution_add_fusion) | copy-start | bytes 786436
Sparse Core Ops, SparseCore 0:
  24.9 76.8 reduce-scatter.3
where the time goes:
time: 217 us
  waiting for transfers between devices  63 us (29%)
  local copies, waits for them, and re-layouts  35.4 us (16%)
  matrix products  29 us (13%)
  blocking collectives  25.4 us (12%)
  other arithmetic  24.7 us (11%)
  starting transfers between devices  21.3 us (10%)
  between operations  17.9 us (8%)
    unnamed x2, waiting for transfers between devices  61.8 us
    dot_general x1, matrix products, shards(): mixed = jnp.einsum('xyc,cd->xyd', parent, parent_mix, precision=HIGH)  27 us
    all_gather x1, blocking collectives, shards(): piece = lax.all_gather(own_values, 'tiles', axis=0, tiled=True)  25.4 us
    unnamed x4, other arithmetic  15.1 us
    gather x2, local copies, waits for them, and re-layouts, shards(): parent_new[jnp.clip(prow, 0, tile_rows - 1)[:, None], jnp.clip(pcol, 0, t...  14.5 us
    ppermute x3, starting transfers between devices, passed_along(): return lax.ppermute(block, axis, route)  10.6 us
    unnamed x17, local copies, waits for them, and re-layouts  8.47 us
    ppermute x2, starting transfers between devices, with_halo(): lax.ppermute(lax.slice_in_dim(block, block.shape[dim] - width, None, axis...  5.75 us
  transfers between devices with their start and end apart: 8, of which 2 were waited for; matrix products, arithmetic and copies ran while one was open for 33% of the time, Pallas kernels for 0%

commit v1 on v0

--- a/solution.py
+++ b/solution.py
@@ -100,7 +100,9 @@
     own_values = jnp.where((row_live[:, None] & col_live[None, :])[..., None], own_values, 0.0)
     pcol = (anchor[1] + ys) // 3 - column_index * tile_cols
     col_ok = col_live & (pcol >= 0) & (pcol < tile_cols)
-    piece = lax.all_gather(own_values, "tiles", axis=0, tiled=True)
+    piece = jnp.concatenate(
+        lax.all_to_all(jnp.stack([own_values] * lax.axis_size("tiles")), "tiles", 0, 0), axis=0
+    )
     slot_index = jnp.arange(piece.shape[0], dtype=jnp.int32)
     sender = slot_index // fb_rows
     sender_base = sender * nest_rows

time: 217 us -> 210 us (0.968)
  blocking collectives: 25.4 us -> 0 us
  waiting for transfers between devices: 63 us -> 70.5 us
  starting transfers between devices: 21.3 us -> 28.6 us
    all_gather x1 -> x0, blocking collectives: 25.4 us -> none  [shards(): piece = lax.all_gather(own_values, 'tiles', axis=0, tiled=True)]
    unnamed x2, waiting for transfers between devices: 61.8 us -> 69.3 us
    all_to_all x0 -> x1, starting transfers between devices: none -> 7.09 us  [shards(): lax.all_to_all(jnp.stack([own_values] * lax.axis_size('tiles')), 'tiles',...]
  transfers between devices with their start and end apart: 8 -> 9, of which waited for: 2 -> 2; matrix products, arithmetic and copies ran while one was open for 33% -> 36% of each run, Pallas kernels for 0% -> 0%
where the time goes in v1:
time: 210 us; the launch traced here: 208 us
  waiting for transfers between devices  70.5 us (34%)
  local copies, waits for them, and re-layouts  36.7 us (17%)
  matrix products  29 us (14%)
  starting transfers between devices  28.6 us (14%)
  other arithmetic  24.9 us (12%)
  between operations  18.1 us (9%)
    unnamed x2, waiting for transfers between devices  69.3 us
    dot_general x1, matrix products, shards(): mixed = jnp.einsum('xyc,cd->xyd', parent, parent_mix, precision=HIGH)  27 us
    unnamed x4, other arithmetic  15.1 us
    gather x2, local copies, waits for them, and re-layouts, shards(): parent_new[jnp.clip(prow, 0, tile_rows - 1)[:, None], jnp.clip(pcol, 0, t...  14.5 us
    ppermute x3, starting transfers between devices, passed_along(): return lax.ppermute(block, axis, route)  10.7 us
    unnamed x17, local copies, waits for them, and re-layouts  8.47 us
    all_to_all x1, starting transfers between devices, shards(): lax.all_to_all(jnp.stack([own_values] * lax.axis_size('tiles')), 'tiles',...  7.09 us
    ppermute x2, starting transfers between devices, with_halo(): lax.ppermute(lax.slice_in_dim(block, block.shape[dim] - width, None, axis...  5.75 us
  transfers between devices with their start and end apart: 9, of which 2 were waited for; matrix products, arithmetic and copies ran while one was open for 36% of the time, Pallas kernels for 0%

profile of v1, /device:TPU:6, one launch (start us, length us, event | category | flops | bytes accessed | tf_op | source)
XLA Modules:
  0.0 207.7 jit_solution(4750958470445217293)
XLA Ops:
  7.2 0.0 copy-start
  7.2 0.0 copy-start.6
  7.2 0.0 copy-start.5
  7.2 0.0 reduce-scatter.4.cloned.1.call-start
  7.3 1.1 fusion.73
  8.3 3.8 %collective-permute-start.1 = (f32[1,256,128]{2,1,0:T(8,128)S(1)}, f32[1,256,128]{2,1,0:T(8,128)S(1)}, u32[]{:S(2)}, u32[]{:S(2)}) collective-permute-start(f32[1,256,128]{2,1,0:T(8,128)S(1)} %get-tuple-element.13), channel_id=1, source_target_pairs={{0,8},{8,16},{16,24},{24,32},{32,40},{40,48},{48,56},{56,64},{64,7... | collective-permute-start | bytes 393224 | tf_op jit(solution)/shard_map/ppermute | solution.py:17
  12.2 1.3 collective-permute-start
  13.5 1.4 fusion.74
  17.7 0.7 and_select_fusion.3
  18.3 0.1 compare_select_fusion.1
  18.4 0.1 fusion.46
  18.5 2.0 constant_dynamic-slice_fusion
  20.5 0.1 reshape.539
  20.6 1.8 gather_fusion
  22.4 2.7 %broadcast_select_fusion = f32[16,3,64,128]{3,2,1,0:T(8,128)} fusion(f32[16,3,64,128]{3,2,1,0:T(8,128)} %bitcast.66, pred[16,3]{1,0:T(8,128)(4,1)S(1)} %fusion.46), kind=kLoop, calls=%fused_computation.30 | loop fusion | flops 393216 | bytes 3145776 | tf_op jit(solution)/shard_map/jit(_where)/select_n | solution.py:73
  25.1 0.0 reduce-scatter.4.cloned.1.call-update
  25.1 0.7 clamp_shift-left_fusion
  25.8 0.7 fusion.60
  26.5 0.7 compare_and_fusion
  27.9 0.7 broadcast_subtract_fusion.1
  28.6 0.7 fusion.54
  29.3 0.7 broadcast_add_fusion
  30.0 0.7 fusion.55
  30.8 0.7 compare_and_fusion.1
  31.5 0.1 compare_select_fusion
  31.5 0.1 multiply_reduce_fusion
  31.6 0.1 and_reduce_fusion
  31.7 0.1 broadcast_and_fusion.1
  31.8 0.1 broadcast_and_fusion
  31.9 0.1 broadcast_or_fusion
  32.0 0.1 reshape.583
  32.1 0.1 reshape.577
  32.2 0.7 constant_dynamic-update-slice_fusion.2
  32.9 69.2 %reduce-scatter.4.cloned.1.call-done = f32[1,3,64,128]{3,2,1,0:T(8,128)} async-done(((f32[16,3,64,128]{3,2,1,0:T(8,128)}), f32[1,3,64,128]{3,2,1,0:T(8,128)}) %reduce-scatter.4.cloned.1.call-update) | async-done | bytes 98320
  102.1 1.4 gather_fusion.1
  103.6 1.4 gather_fusion.2
  105.0 0.4 convolution_multiply_fusion.1
  105.5 0.4 fusion.10
  105.9 0.0 copy-start.1
  105.9 3.2 %collective-permute-start.4 = (f32[1,128,128]{2,1,0:T(8,128)S(1)}, f32[1,128,128]{2,1,0:T(8,128)S(1)}, u32[]{:S(2)}, u32[]{:S(2)}) collective-permute-start(f32[1,128,128]{2,1,0:T(8,128)S(1)} %slice.129), channel_id=1, source_target_pairs={{0,8},{8,16},{16,24},{24,32},{32,40},{40,48},{48,56},{56,64},{64,7... | collective-permute-start | bytes 196616 | tf_op jit(solution)/shard_map/ppermute | solution.py:28
  109.1 7.7 %constant_dynamic-update-slice_fusion.1 = f32[66,256,128]{2,1,0:T(8,128)} fusion(f32[66,256,128]{2,1,0:T(8,128)} %constant_dynamic-update-slice_fusion.2, f32[64,256,128]{2,1,0:T(8,128)} %param.6), kind=kLoop, calls=%fused_computation.90 | loop fusion | bytes 16777216
  116.9 0.4 convolution_add_fusion.2
  117.2 3.3 %collective-permute-start.5 = (f32[1,128,128]{2,1,0:T(8,128)S(1)}, f32[1,128,128]{2,1,0:T(8,128)S(1)}, u32[]{:S(2)}, u32[]{:S(2)}) collective-permute-start(f32[1,128,128]{2,1,0:T(8,128)S(1)} %slice.133), channel_id=1, source_target_pairs={{0,8},{8,16},{16,24},{24,32},{32,40},{40,48},{48,56},{56,64},{64,7... | collective-permute-start | bytes 196616 | tf_op jit(solution)/shard_map/ppermute | solution.py:28
  120.6 0.7 constant_dynamic-update-slice_fusion
  121.2 1.2 collective-permute-done.5
  122.4 0.4 convolution_add_fusion.1
  122.8 4.3 %collective-permute-start.6 = (f32[1,128,128]{2,1,0:T(8,128)S(1)}, f32[1,128,128]{2,1,0:T(8,128)S(1)}, u32[]{:S(2)}, u32[]{:S(2)}) collective-permute-start(f32[1,128,128]{2,1,0:T(8,128)S(1)} %slice.136), channel_id=1, source_target_pairs={{0,8},{8,16},{16,24},{24,32},{32,40},{40,48},{48,56},{56,64},{64,7... | collective-permute-start | bytes 196616 | tf_op jit(solution)/shard_map/ppermute | solution.py:28
  127.1 1.1 fusion.72
  128.2 1.9 collective-permute-start.3
  130.1 3.6 %collective-permute-start.2 = (f32[66,1,128]{2,1,0:T(1,128)S(1)}, f32[66,1,128]{2,1,0:T(1,128)S(1)}, u32[]{:S(2)}, u32[]{:S(2)}) collective-permute-start(f32[66,1,128]{2,1,0:T(1,128)S(1)} %get-tuple-element.10), channel_id=1, source_target_pairs={{1,0},{2,1},{3,2},{4,3},{5,4},{6,5},{7,6},{9,8},{10,9},{11,10},{12... | collective-permute-start | bytes 101384 | tf_op jit(solution)/shard_map/ppermute | solution.py:20
  133.8 0.4 convolution_add_fusion
  134.2 0.6 gather_fusion.3
  134.8 0.1 copy.10
  134.9 0.6 gather_fusion.4
  135.5 0.1 bitcast_select_fusion
  135.6 1.1 stack.2
  136.7 7.1 %all-to-all-start = ((f32[16,2,43,128]{3,1,2,0:T(2,128)}), f32[16,2,43,128]{3,1,2,0:T(2,128)S(1)}, u32[]{:S(2)}, u32[]{:S(2)}) async-start(f32[16,2,43,128]{3,1,2,0:T(2,128)} %stack.2), calls=%async_computation | async-start | bytes 1409024 | tf_op jit(solution)/shard_map/all_to_all | solution.py:104
  143.9 27.0 %fusion.4 = f32[64,256,128]{2,1,0:T(8,128)} fusion(f32[64,256,128]{2,1,0:T(8,128)} %param.6, f32[66,256,128]{2,1,0:T(8,128)} %constant_dynamic-update-slice_fusion, f32[66,1,128]{2,1,0:T(1,128)S(1)} %collective-permute-done.3, f32[66,1,128]{2,1,0:T(1,128)S(1)} %collective-permute-done.2, f32[1,256,128]{2,1,0:T(8,128)S(1)} %collective-permute-done.1, ...), kind=kOutput, calls=%fused_computation.12 | convolution fusion | flops 3246391296 | bytes 25823232 | tf_op jit(solution)/shard_map/xyc,cd->xyd/dot_general | solution.py:77
  170.9 14.5 %gather_fusion.5 = f32[1376,128]{1,0:T(8,128)S(1)} fusion(f32[64,256,128]{2,1,0:T(8,128)} %fusion.4, s32[1376]{0:T(1024)S(1)} %reshape.577), kind=kCustom, calls=%fused_computation.5 | custom fusion | bytes 1420032 | tf_op jit(solution)/shard_map/gather | solution.py:113
  185.4 0.1 reshape.580
  185.5 0.1 copy.11
  185.6 0.3 fusion.12
  185.8 0.1 reshape.585
  185.9 14.9 %scatter_fusion = f32[16384,128]{1,0:T(8,128)} fusion(f32[16384,128]{1,0:T(8,128)} %bitcast.64, s32[1376]{0:T(1024)S(1)} %reshape.583, f32[1376,128]{1,0:T(8,128)S(1)} %reshape.585), kind=kCustom, calls=%fused_computation.6 | custom fusion | flops 176128 | bytes 2119040
  (40 shorter events, 0.2 us)
Async XLA Ops:
  7.2 136.7 %copy-start = (f32[128,128]{1,0:T(8,128)S(1)}, f32[128,128]{1,0:T(8,128)}, u32[]{:S(2)}) copy-start(f32[128,128]{1,0:T(8,128)} %param.8) | copy-start | bytes 196612
  7.2 24.4 %copy-start.6 = (s32[2]{0:T(128)S(1)}, s32[2]{0:T(128)}, u32[]{:S(2)}) copy-start(s32[2]{0:T(128)} %constant.162) | copy-start | bytes 28
  7.2 24.4 %copy-start.5 = (s32[2]{0:T(128)S(1)}, s32[2]{0:T(128)}, u32[]{:S(2)}) copy-start(s32[2]{0:T(128)} %constant.165) | copy-start | bytes 28
  7.2 24.5 %copy-start.4 = (f32[2,128]{1,0:T(2,128)S(1)}, f32[2,128]{1,0:T(2,128)}, u32[]{:S(2)}) copy-start(f32[2,128]{1,0:T(2,128)} %param.10) | copy-start | bytes 3076
  7.2 98.2 %copy-start.3 = (f32[1,4,128,128]{3,2,1,0:T(8,128)S(1)}, f32[1,4,128,128]{3,2,1,0:T(8,128)}, u32[]{:S(2)}) copy-start(f32[1,4,128,128]{3,2,1,0:T(8,128)} %param.7) | copy-start | bytes 786436
  7.2 94.9 %reduce-scatter.4.cloned.1.call-start = ((), (), s32[]{:S(2)}) async-start(), calls=%async_computation.2 | async-start | bytes 1671168
  8.3 23.9 %collective-permute-start.1 = (f32[1,256,128]{2,1,0:T(8,128)S(1)}, f32[1,256,128]{2,1,0:T(8,128)S(1)}, u32[]{:S(2)}, u32[]{:S(2)}) collective-permute-start(f32[1,256,128]{2,1,0:T(8,128)S(1)} %get-tuple-element.13), channel_id=1, source_target_pairs={{0,8},{8,16},{16,24},{24,32},{32,40},{40,48},{48,56},{56,64},{64,7... | collective-permute-start | bytes 393224 | tf_op jit(solution)/shard_map/ppermute | solution.py:17
  12.2 108.4 %collective-permute-start = (f32[1,256,128]{2,1,0:T(8,128)S(1)}, f32[1,256,128]{2,1,0:T(8,128)S(1)}, u32[]{:S(2)}, u32[]{:S(2)}) collective-permute-start(f32[1,256,128]{2,1,0:T(8,128)S(1)} %get-tuple-element.12), channel_id=1, source_target_pairs={{8,0},{16,8},{24,16},{32,24},{40,32},{48,40},{56,48},{64,56},{72,6... | collective-permute-start | bytes 393224 | tf_op jit(solution)/shard_map/ppermute | solution.py:20
  105.9 10.9 %copy-start.1 = (f32[128,128]{1,0:T(8,128)S(1)}, f32[128,128]{1,0:T(8,128)}, u32[]{:S(2)}) copy-start(f32[128,128]{1,0:T(8,128)} %param.9) | copy-start | bytes 196612
  105.9 10.9 %collective-permute-start.4 = (f32[1,128,128]{2,1,0:T(8,128)S(1)}, f32[1,128,128]{2,1,0:T(8,128)S(1)}, u32[]{:S(2)}, u32[]{:S(2)}) collective-permute-start(f32[1,128,128]{2,1,0:T(8,128)S(1)} %slice.129), channel_id=1, source_target_pairs={{0,8},{8,16},{16,24},{24,32},{32,40},{40,48},{48,56},{56,64},{64,7... | collective-permute-start | bytes 196616 | tf_op jit(solution)/shard_map/ppermute | solution.py:28
  117.2 5.2 %collective-permute-start.5 = (f32[1,128,128]{2,1,0:T(8,128)S(1)}, f32[1,128,128]{2,1,0:T(8,128)S(1)}, u32[]{:S(2)}, u32[]{:S(2)}) collective-permute-start(f32[1,128,128]{2,1,0:T(8,128)S(1)} %slice.133), channel_id=1, source_target_pairs={{0,8},{8,16},{16,24},{24,32},{32,40},{40,48},{48,56},{56,64},{64,7... | collective-permute-start | bytes 196616 | tf_op jit(solution)/shard_map/ppermute | solution.py:28
  122.8 11.0 %collective-permute-start.6 = (f32[1,128,128]{2,1,0:T(8,128)S(1)}, f32[1,128,128]{2,1,0:T(8,128)S(1)}, u32[]{:S(2)}, u32[]{:S(2)}) collective-permute-start(f32[1,128,128]{2,1,0:T(8,128)S(1)} %slice.136), channel_id=1, source_target_pairs={{0,8},{8,16},{16,24},{24,32},{32,40},{40,48},{48,56},{56,64},{64,7... | collective-permute-start | bytes 196616 | tf_op jit(solution)/shard_map/ppermute | solution.py:28
  128.2 15.6 %collective-permute-start.3 = (f32[66,1,128]{2,1,0:T(1,128)S(1)}, f32[66,1,128]{2,1,0:T(1,128)S(1)}, u32[]{:S(2)}, u32[]{:S(2)}) collective-permute-start(f32[66,1,128]{2,1,0:T(1,128)S(1)} %get-tuple-element.11), channel_id=1, source_target_pairs={{0,1},{1,2},{2,3},{3,4},{4,5},{5,6},{6,7},{8,9},{9,10},{10,11},{11... | collective-permute-start | bytes 101384 | tf_op jit(solution)/shard_map/ppermute | solution.py:17
  130.1 13.7 %collective-permute-start.2 = (f32[66,1,128]{2,1,0:T(1,128)S(1)}, f32[66,1,128]{2,1,0:T(1,128)S(1)}, u32[]{:S(2)}, u32[]{:S(2)}) collective-permute-start(f32[66,1,128]{2,1,0:T(1,128)S(1)} %get-tuple-element.10), channel_id=1, source_target_pairs={{1,0},{2,1},{3,2},{4,3},{5,4},{6,5},{7,6},{9,8},{10,9},{11,10},{12... | collective-permute-start | bytes 101384 | tf_op jit(solution)/shard_map/ppermute | solution.py:20
  134.2 36.7 %copy-start.2 = (f32[4,128,128]{2,1,0:T(8,128)}, f32[4,128,128]{2,1,0:T(8,128)S(1)}, u32[]{:S(2)}) copy-start(f32[4,128,128]{2,1,0:T(8,128)S(1)} %convolution_add_fusion) | copy-start | bytes 786436
  136.7 48.7 %all-to-all-start = ((f32[16,2,43,128]{3,1,2,0:T(2,128)}), f32[16,2,43,128]{3,1,2,0:T(2,128)S(1)}, u32[]{:S(2)}, u32[]{:S(2)}) async-start(f32[16,2,43,128]{3,1,2,0:T(2,128)} %stack.2), calls=%async_computation | async-start | bytes 1409024 | tf_op jit(solution)/shard_map/all_to_all | solution.py:104
Sparse Core Ops, SparseCore 0:
  25.3 76.8 reduce-scatter.3
